TPU v7x, 512 devices: a whole 4x4x16 slice. The times are simulated.
512 devices in a mesh: dp: 8 (over z_hi, x), row: 8 (over y, core), col: 8 (over z_lo).
Axes of the slice: x: 4, y: 4, z: 16 (z_hi: 2, z_lo: 8; z = z_hi * 8 + z_lo), core: 2. Of those that a mesh axis runs over, the one named last changes fastest.
Arguments:
- tokens: bfloat16 [65536, 8192], P(('dp', 'row', 'col')), parts along dimension 0, may hold values from -60 to 60
- norm_gain: float32 [8192], replicated, may hold values from 0.1 to 1.9
- w_key: bfloat16 [8192, 1024], P('row', 'col'), may hold values from -0.0625 to 0.0625
- w_value: bfloat16 [8192, 1024], P('row', 'col'), may hold values from -0.0625 to 0.0625
Outputs:
- key_rows: bfloat16 [65536, 1024], P(('dp', 'row', 'col')), parts along dimension 0
- value_rows: bfloat16 [65536, 1024], P(('dp', 'row', 'col')), parts along dimension 0
There are 8 independent parts, one for each index of `dp`. A program takes and returns all parts, laid end to end along the dimension named above; an argument that names none is the same for every part. Nothing has to cross between parts.
All inputs are finite; a program needn't handle non-finite values.
Results may differ from a plain program's by a relative error of at most 0.014.
Values may be sent and summed in bfloat16 or wider, within the bound.
A program may use at most 64 MiB of HBM per device.

v0:
```python
import jax
import jax.numpy as jnp
from jax import lax
from jax.sharding import PartitionSpec as P

HEAD = 128
rope_base = 500000.0


def rotate(projected, positions):
    row_count = projected.shape[0]
    head_count = projected.shape[1] // HEAD
    half_head = HEAD // 2
    frequency = rope_base ** (-2.0 * jnp.arange(half_head, dtype=jnp.float32) / HEAD)
    angles = positions.astype(jnp.float32)[:, None] * frequency[None, :]
    cosine = jnp.cos(angles)[:, None, :]
    sine = jnp.sin(angles)[:, None, :]
    split_heads = projected.reshape(row_count, head_count, HEAD)
    first = split_heads[:, :, :half_head]
    second = split_heads[:, :, half_head:]
    turned = jnp.concatenate(
        [first * cosine - second * sine, second * cosine + first * sine], axis=2
    )
    return turned.reshape(row_count, head_count * HEAD)


def body(tokens, norm_gain, w_key, w_value):
    col_count = lax.axis_size("col")
    row_index = lax.axis_index("row")
    col_index = lax.axis_index("col")
    own_rows = tokens.shape[0]
    widened = tokens.astype(jnp.float32)
    inverse_rms = lax.rsqrt(jnp.mean(widened * widened, axis=1, keepdims=True) + 1e-05)
    normed = (widened * inverse_rms * norm_gain[None, :]).astype(jnp.bfloat16)
    tile = lax.all_to_all(normed, "row", split_axis=1, concat_axis=0, tiled=True)
    key_weights, value_weights = (
        lax.all_gather(w_key, "col", axis=1, tiled=True),
        lax.all_gather(w_value, "col", axis=1, tiled=True),
    )
    key_part = jnp.dot(tile, key_weights, preferred_element_type=jnp.float32)
    value_part = jnp.dot(tile, value_weights, preferred_element_type=jnp.float32)
    key_sum, value_sum = (
        lax.psum_scatter(
            key_part.astype(jnp.bfloat16), "row", scatter_dimension=0, tiled=True
        ).astype(jnp.float32),
        lax.psum_scatter(
            value_part.astype(jnp.bfloat16), "row", scatter_dimension=0, tiled=True
        ).astype(jnp.float32),
    )
    positions = (row_index * col_count + col_index) * own_rows + jnp.arange(
        own_rows, dtype=jnp.int32
    )
    key_rows = rotate(key_sum, positions).astype(jnp.bfloat16)
    value_rows = value_sum.astype(jnp.bfloat16)
    return (key_rows, value_rows)


def solution(mesh):
    placed = (P(("dp", "row", "col"), None), P(), P("row", "col"), P("row", "col"))
    return jax.shard_map(
        body,
        mesh=mesh,
        in_specs=placed,
        out_specs=(P(("dp", "row", "col"), None), P(("dp", "row", "col"), None)),
        check_vma=False,
    )
```

profile of v0, /device:TPU:2, one launch (start us, length us, event | category | flops | bytes accessed | tf_op | source)
XLA Modules:
  0.0 248.9 jit_solution(14497560311085529130)
XLA Ops:
  7.2 0.0 all-gather.3.cloned.1.call-start
  7.2 0.7 all-gather.3.cloned.1.call-update
  7.9 0.0 all-gather.5.cloned.1.call-start
  7.9 0.7 all-gather.5.cloned.1.call-update
  8.6 0.0 reduce-scatter.3.cloned.1.call-start
  8.7 3.2 %copy.6 = bf16[128,8192]{0,1:T(8,128)(2,1)S(1)} copy(bf16[128,8192]{1,0:T(8,128)(2,1)} %param.4) | data formatting | bytes 4194304 | tf_op args[0]
  11.9 0.0 copy-start.1
  11.9 1.1 fusion
  13.0 0.0 copy-done.1
  13.0 3.5 %fusion.2 = bf16[128,8192]{0,1:T(8,128)(2,1)S(1)} fusion(bf16[128,8192]{0,1:T(8,128)(2,1)S(1)} %copy.6, f32[8192]{0:T(1024)S(1)} %copy-done.1, f32[128]{0:T(128)S(1)} %add_rsqrt_fusion), kind=kLoop, calls=%fused_computation.4 | loop fusion | flops 4194304 | bytes 4227584 | tf_op jit(solution)/shard_map/convert_element_type | solution.py:34
  16.5 31.8 %all_to_all.19 = bf16[128,8,1024]{0,2,1:T(8,128)(2,1)S(1)} all-to-all(bf16[128,8,1024]{0,2,1:T(8,128)(2,1)S(1)} %bitcast.14), channel_id=1, replica_groups=mesh['dp'=8,'row'=8,'col'=8] {'row'}, dimensions={1} | all-to-all | bytes 4194304 | tf_op jit(solution)/shard_map/all_to_all | solution.py:35
  48.3 2.6 %copy.7 = bf16[8,128,1024]{2,1,0:T(8,128)(2,1)} copy(bf16[8,128,1024]{1,2,0:T(8,128)(2,1)S(1)} %bitcast.15) | data formatting | bytes 4194304 | tf_op jit(solution)/shard_map/all_to_all | solution.py:35
  50.9 37.4 %all-gather.3.cloned.1.call-done = bf16[1024,1024]{1,0:T(8,128)(2,1)} async-done(((bf16[1024,128]{1,0:T(8,128)(2,1)}), bf16[1024,1024]{1,0:T(8,128)(2,1)}) %all-gather.3.cloned.1.call-update) | async-done | bytes 2097168 | tf_op jit(solution)/shard_map/all_gather | solution.py:37
  88.3 5.9 %convolution_convert_fusion.1 = bf16[1024,1024]{1,0:T(8,128)(2,1)} fusion(bf16[1024,1024]{1,0:T(8,128)(2,1)} %bitcast.17, bf16[1024,1024]{1,0:T(8,128)(2,1)} %all-gather.3.cloned.1.call-done), kind=kOutput, calls=%fused_computation.6 | convolution fusion | flops 2148532224 | bytes 6291456 | tf_op jit(solution)/shard_map/dot_general | solution.py:40
  94.2 0.0 copy-start
  94.2 0.0 reduce-scatter.3.cloned.1.call-update
  94.2 0.0 reduce-scatter.5.cloned.1.call-start
  94.3 65.2 %all-gather.5.cloned.1.call-done = bf16[1024,1024]{1,0:T(8,128)(2,1)} async-done(((bf16[1024,128]{1,0:T(8,128)(2,1)}), bf16[1024,1024]{1,0:T(8,128)(2,1)}) %all-gather.5.cloned.1.call-update) | async-done | bytes 2097168 | tf_op jit(solution)/shard_map/all_gather | solution.py:38
  159.4 0.0 copy-done
  159.5 5.3 %convolution_convert_fusion = bf16[1024,1024]{1,0:T(8,128)(2,1)} fusion(bf16[1024,1024]{1,0:T(8,128)(2,1)S(1)} %bitcast.18, bf16[1024,1024]{1,0:T(8,128)(2,1)} %all-gather.5.cloned.1.call-done), kind=kOutput, calls=%fused_computation.5 | convolution fusion | flops 2148532224 | bytes 6291456 | tf_op jit(solution)/shard_map/dot_general | solution.py:41
  164.7 0.0 reduce-scatter.5.cloned.1.call-update
  164.8 0.3 multiply_cosine_fusion
  165.1 33.8 %reduce-scatter.3.cloned.1.call-done = bf16[128,1024]{1,0:T(8,128)(2,1)} async-done(((bf16[1024,1024]{1,0:T(8,128)(2,1)}), bf16[128,1024]{1,0:T(8,128)(2,1)}) %reduce-scatter.3.cloned.1.call-update) | async-done | bytes 262160 | tf_op jit(solution)/shard_map/reduce_scatter | solution.py:43
  198.9 1.0 convert_bitcast_fusion
  199.9 0.1 copy.8
  200.0 0.3 subtract_convert_fusion
  200.3 0.1 pad_maximum_fusion
  200.4 0.8 copy.11
  201.2 41.2 %reduce-scatter.5.cloned.1.call-done = bf16[128,1024]{1,0:T(8,128)(2,1)} async-done(((bf16[1024,1024]{1,0:T(8,128)(2,1)}), bf16[128,1024]{1,0:T(8,128)(2,1)}) %reduce-scatter.5.cloned.1.call-update) | async-done | bytes 262160 | tf_op jit(solution)/shard_map/reduce_scatter | solution.py:46
  (3 shorter events, 0.0 us)
Async XLA Ops:
  7.2 81.2 %all-gather.3.cloned.1.call-start = ((), (), s32[]{:S(2)}) async-start(), calls=%async_computation.3 | async-start | bytes 2359296 | tf_op jit(solution)/shard_map/all_gather | solution.py:37
  7.9 151.6 %all-gather.5.cloned.1.call-start = ((), (), s32[]{:S(2)}) async-start(), calls=%async_computation.5 | async-start | bytes 2359296 | tf_op jit(solution)/shard_map/all_gather | solution.py:38
  8.6 190.2 %reduce-scatter.3.cloned.1.call-start = ((), (), s32[]{:S(2)}) async-start(), calls=%async_computation.4 | async-start | bytes 2359296 | tf_op jit(solution)/shard_map/reduce_scatter | solution.py:43
  11.9 1.1 copy-start.1
  94.2 65.3 %copy-start = (bf16[8,128,1024]{2,1,0:T(8,128)(2,1)S(1)}, bf16[8,128,1024]{2,1,0:T(8,128)(2,1)}, u32[]{:S(2)}) copy-start(bf16[8,128,1024]{2,1,0:T(8,128)(2,1)} %copy.7) | copy-start | bytes 6291460
  94.2 148.2 %reduce-scatter.5.cloned.1.call-start = ((), (), s32[]{:S(2)}) async-start(), calls=%async_computation.6 | async-start | bytes 2359296 | tf_op jit(solution)/shard_map/reduce_scatter | solution.py:46
Sparse Core Ops, SparseCore 0:
  10.0 78.2 all-gather.2
  90.3 69.0 all-gather.4
  162.3 36.5 reduce-scatter.2
  202.2 40.1 reduce-scatter.4
where the time goes:
time: 249 us
  waiting for transfers between devices  179 us (72%)
  blocking collectives  31.8 us (13%)
  between operations  13.8 us (6%)
  matrix products  11.1 us (4%)
  local copies, waits for them, and re-layouts  6.71 us (3%)
  other arithmetic  6.31 us (3%)
    all_gather x1, waiting for transfers between devices, body(): lax.all_gather(w_value, 'col', axis=1, tiled=True)  65.2 us
    reduce_scatter x1, waiting for transfers between devices, body(): lax.psum_scatter(value_part.astype(jnp.bfloat16), 'row', scatter_dimensio...  41.2 us
    all_gather x1, waiting for transfers between devices, body(): lax.all_gather(w_key, 'col', axis=1, tiled=True)  37.4 us
    reduce_scatter x1, waiting for transfers between devices, body(): lax.psum_scatter(key_part.astype(jnp.bfloat16), 'row', scatter_dimension=...  33.8 us
    all_to_all x1, blocking collectives, body(): lax.all_to_all(normed, 'row', split_axis=1, concat_axis=0, tiled=True)  31.8 us
    dot_general x1, matrix products, body(): key_part = jnp.dot(tile, key_weights, preferred_element_type=jnp.float32)  5.86 us
    dot_general x1, matrix products, body(): jnp.dot(tile, value_weights, preferred_element_type=jnp.float32)  5.26 us
  transfers between devices with their start and end apart: 4, of which 4 were waited for; matrix products, arithmetic and copies ran while one was open for 10% of the time, Pallas kernels for 0%

commit v1 on v0

--- a/solution.py
+++ b/solution.py
@@ -1,3 +1,4 @@
+import functools
 import jax
 import jax.numpy as jnp
 from jax import lax
@@ -5,6 +6,22 @@
 
 HEAD = 128
 rope_base = 500000.0
+
+
+def trace_modes_on_mesh(message, ax_name):
+    y_new = jnp.concatenate(
+        lax.all_to_all(
+            jnp.stack([message for _ in range(lax.axis_size(ax_name))], 0),
+            ax_name,
+            concat_axis=0,
+            split_axis=0,
+        ),
+        1,
+    )
+    return y_new
+
+
+put_frame = functools.partial(trace_modes_on_mesh, ax_name="col")
 
 
 def rotate(projected, positions):
@@ -35,7 +52,7 @@
     tile = lax.all_to_all(normed, "row", split_axis=1, concat_axis=0, tiled=True)
     key_weights, value_weights = (
         lax.all_gather(w_key, "col", axis=1, tiled=True),
-        lax.all_gather(w_value, "col", axis=1, tiled=True),
+        put_frame(w_value),
     )
     key_part = jnp.dot(tile, key_weights, preferred_element_type=jnp.float32)
     value_part = jnp.dot(tile, value_weights, preferred_element_type=jnp.float32)

time: 249 us -> 279 us (1.12)
  waiting for transfers between devices: 179 us -> 221 us
  blocking collectives: 31.8 us -> 0 us
  starting transfers between devices: 0.16 us -> 17.2 us
    all_gather x1 -> x0, waiting for transfers between devices: 65.2 us -> none  [body(): lax.all_gather(w_value, 'col', axis=1, tiled=True)]
    all_gather x1, waiting for transfers between devices: 37.4 us -> 93.5 us  [body(): lax.all_gather(w_key, 'col', axis=1, tiled=True)]
    all_to_all x0 -> x2, waiting for transfers between devices: none -> 44.5 us  [the longest x1 26.3 us: body(): lax.all_to_all(normed, 'row', split_axis=1, concat_axis=0, tiled=True)]
    all_to_all x1 -> x0, blocking collectives: 31.8 us -> none  [body(): lax.all_to_all(normed, 'row', split_axis=1, concat_axis=0, tiled=True)]
    all_to_all x0 -> x2, starting transfers between devices: none -> 17.1 us  [the longest x1 12.5 us: trace_modes_on_mesh(): lax.all_to_all(jnp.stack([message for _ in range(lax.axis_size(ax_name))]...]
    reduce_scatter x1, waiting for transfers between devices: 33.8 us -> 41.1 us  [body(): lax.psum_scatter(key_part.astype(jnp.bfloat16), 'row', scatter_dimension=...]
  transfers between devices with their start and end apart: 4 -> 5, of which waited for: 4 -> 5; matrix products, arithmetic and copies ran while one was open for 10% -> 7% of each run, Pallas kernels for 0% -> 0%
where the time goes in v1:
time: 279 us
  waiting for transfers between devices  221 us (79%)
  starting transfers between devices  17.2 us (6%)
  between operations  13.8 us (5%)
  matrix products  11.2 us (4%)
  local copies, waits for them, and re-layouts  8.5 us (3%)
  other arithmetic  7.17 us (3%)
    all_gather x1, waiting for transfers between devices, body(): lax.all_gather(w_key, 'col', axis=1, tiled=True)  93.5 us
    reduce_scatter x1, waiting for transfers between devices, body(): lax.psum_scatter(value_part.astype(jnp.bfloat16), 'row', scatter_dimensio...  41.4 us
    reduce_scatter x1, waiting for transfers between devices, body(): lax.psum_scatter(key_part.astype(jnp.bfloat16), 'row', scatter_dimension=...  41.1 us
    all_to_all x1, waiting for transfers between devices, body(): lax.all_to_all(normed, 'row', split_axis=1, concat_axis=0, tiled=True)  26.3 us
    all_to_all x1, waiting for transfers between devices, trace_modes_on_mesh(): lax.all_to_all(jnp.stack([message for _ in range(lax.axis_size(ax_name))]...  18.2 us
    all_to_all x1, starting transfers between devices, trace_modes_on_mesh(): lax.all_to_all(jnp.stack([message for _ in range(lax.axis_size(ax_name))]...  12.5 us
    dot_general x1, matrix products, body(): key_part = jnp.dot(tile, key_weights, preferred_element_type=jnp.float32)  5.87 us
  transfers between devices with their start and end apart: 5, of which 5 were waited for; matrix products, arithmetic and copies ran while one was open for 7% of the time, Pallas kernels for 0%

profile of v1, /device:TPU:2, one launch (start us, length us, event | category | flops | bytes accessed | tf_op | source)
XLA Modules:
  0.0 279.1 jit_solution(5175636371358946661)
XLA Ops:
  7.2 3.2 %copy.7 = bf16[128,8192]{0,1:T(8,128)(2,1)S(1)} copy(bf16[128,8192]{1,0:T(8,128)(2,1)} %param.4) | data formatting | bytes 4194304 | tf_op args[0]
  10.4 0.0 copy-start.2
  10.4 1.1 fusion
  11.5 0.0 copy-done.2
  11.5 4.3 %fusion.2 = bf16[128,8192]{0,1:T(8,128)(2,1)} fusion(bf16[128,8192]{0,1:T(8,128)(2,1)S(1)} %copy.7, f32[8192]{0:T(1024)S(1)} %copy-done.2, f32[128]{0:T(128)S(1)} %add_rsqrt_fusion), kind=kLoop, calls=%fused_computation.4 | loop fusion | flops 4194304 | bytes 4227584 | tf_op jit(solution)/shard_map/convert_element_type | solution.py:51
  15.9 0.0 copy-start.1
  15.9 4.6 %all-to-all-start = ((bf16[128,8,1024]{0,2,1:T(8,128)(2,1)}), bf16[128,8,1024]{0,2,1:T(8,128)(2,1)S(1)}, u32[]{:S(2)}, u32[]{:S(2)}) async-start(bf16[128,8,1024]{0,2,1:T(8,128)(2,1)} %bitcast.18), calls=%async_computation | async-start | bytes 4194304 | tf_op jit(solution)/shard_map/all_to_all | solution.py:52
  20.5 0.0 all-gather.2.cloned.1.call-start
  20.5 0.7 all-gather.2.cloned.1.call-update
  21.2 0.0 copy-done.1
  21.2 0.1 copy.9
  21.4 26.3 %all-to-all-done = bf16[128,8,1024]{0,2,1:T(8,128)(2,1)S(1)} async-done(((bf16[128,8,1024]{0,2,1:T(8,128)(2,1)}), bf16[128,8,1024]{0,2,1:T(8,128)(2,1)S(1)}, u32[]{:S(2)}, u32[]{:S(2)}) %all-to-all-start) | async-done | bytes 2097184 | tf_op jit(solution)/shard_map/all_to_all | solution.py:52
  47.7 1.6 stack.2
  49.3 12.5 %all-to-all-start.1 = ((bf16[8,1024,128]{1,2,0:T(8,128)(2,1)}), bf16[8,1024,128]{1,2,0:T(8,128)(2,1)}, u32[]{:S(2)}, u32[]{:S(2)}) async-start(bf16[8,1024,128]{1,2,0:T(8,128)(2,1)} %stack.2), calls=%async_computation.2 | async-start | bytes 4194304 | tf_op jit(solution)/shard_map/all_to_all | solution.py:13
  61.8 0.0 reduce-scatter.3.cloned.1.call-start
  61.9 2.7 copy.8
  64.5 93.5 %all-gather.2.cloned.1.call-done = bf16[1024,1024]{1,0:T(8,128)(2,1)} async-done(((bf16[1024,128]{1,0:T(8,128)(2,1)}), bf16[1024,1024]{1,0:T(8,128)(2,1)}) %all-gather.2.cloned.1.call-update) | async-done | bytes 2097168 | tf_op jit(solution)/shard_map/all_gather | solution.py:54
  158.0 5.9 %convolution_convert_fusion.1 = bf16[1024,1024]{1,0:T(8,128)(2,1)} fusion(bf16[1024,1024]{1,0:T(8,128)(2,1)} %bitcast.20, bf16[1024,1024]{1,0:T(8,128)(2,1)} %all-gather.2.cloned.1.call-done), kind=kOutput, calls=%fused_computation.6 | convolution fusion | flops 2148532224 | bytes 6291456 | tf_op jit(solution)/shard_map/dot_general | solution.py:57
  163.9 0.0 reduce-scatter.3.cloned.1.call-update
  163.9 0.0 reduce-scatter.5.cloned.1.call-start
  164.0 18.2 %all-to-all-done.1 = bf16[8,1024,128]{1,2,0:T(8,128)(2,1)} async-done(((bf16[8,1024,128]{1,2,0:T(8,128)(2,1)}), bf16[8,1024,128]{1,2,0:T(8,128)(2,1)}, u32[]{:S(2)}, u32[]{:S(2)}) %all-to-all-start.1) | async-done | bytes 2097184 | tf_op jit(solution)/shard_map/all_to_all | solution.py:13
  182.1 0.0 copy-done
  182.1 5.3 %convolution_convert_fusion = bf16[1024,1024]{1,0:T(8,128)(2,1)} fusion(bf16[1024,1024]{1,0:T(8,128)(2,1)S(1)} %bitcast.21, bf16[1024,1024]{0,1:T(8,128)(2,1)} %bitcast.4), kind=kOutput, calls=%fused_computation.5 | convolution fusion | flops 2148532224 | bytes 6291456 | tf_op jit(solution)/shard_map/dot_general | solution.py:58
  187.4 0.0 reduce-scatter.5.cloned.1.call-update
  187.5 0.3 multiply_cosine_fusion
  187.8 41.1 %reduce-scatter.3.cloned.1.call-done = bf16[128,1024]{1,0:T(8,128)(2,1)} async-done(((bf16[1024,1024]{1,0:T(8,128)(2,1)}), bf16[128,1024]{1,0:T(8,128)(2,1)}) %reduce-scatter.3.cloned.1.call-update) | async-done | bytes 262160 | tf_op jit(solution)/shard_map/reduce_scatter | solution.py:60
  228.9 1.0 convert_bitcast_fusion
  229.9 0.1 copy.10
  230.0 0.3 subtract_convert_fusion
  230.2 0.1 pad_maximum_fusion
  230.4 0.8 copy.13
  231.2 41.4 %reduce-scatter.5.cloned.1.call-done = bf16[128,1024]{1,0:T(8,128)(2,1)} async-done(((bf16[1024,1024]{1,0:T(8,128)(2,1)}), bf16[128,1024]{1,0:T(8,128)(2,1)}) %reduce-scatter.5.cloned.1.call-update) | async-done | bytes 262160 | tf_op jit(solution)/shard_map/reduce_scatter | solution.py:63
  (4 shorter events, 0.0 us)
Async XLA Ops:
  10.4 1.1 copy-start.2
  15.9 5.3 %copy-start.1 = (bf16[1024,128]{1,0:T(8,128)(2,1)S(1)}, bf16[1024,128]{1,0:T(8,128)(2,1)}, u32[]{:S(2)}) copy-start(bf16[1024,128]{1,0:T(8,128)(2,1)} %param.7) | copy-start | bytes 786436
  15.9 31.8 %all-to-all-start = ((bf16[128,8,1024]{0,2,1:T(8,128)(2,1)}), bf16[128,8,1024]{0,2,1:T(8,128)(2,1)S(1)}, u32[]{:S(2)}, u32[]{:S(2)}) async-start(bf16[128,8,1024]{0,2,1:T(8,128)(2,1)} %bitcast.18), calls=%async_computation | async-start | bytes 4194304 | tf_op jit(solution)/shard_map/all_to_all | solution.py:52
  20.5 137.5 %all-gather.2.cloned.1.call-start = ((), (), s32[]{:S(2)}) async-start(), calls=%async_computation.4 | async-start | bytes 2359296 | tf_op jit(solution)/shard_map/all_gather | solution.py:54
  49.3 132.9 %all-to-all-start.1 = ((bf16[8,1024,128]{1,2,0:T(8,128)(2,1)}), bf16[8,1024,128]{1,2,0:T(8,128)(2,1)}, u32[]{:S(2)}, u32[]{:S(2)}) async-start(bf16[8,1024,128]{1,2,0:T(8,128)(2,1)} %stack.2), calls=%async_computation.2 | async-start | bytes 4194304 | tf_op jit(solution)/shard_map/all_to_all | solution.py:13
  61.8 167.1 %reduce-scatter.3.cloned.1.call-start = ((), (), s32[]{:S(2)}) async-start(), calls=%async_computation.5 | async-start | bytes 2359296 | tf_op jit(solution)/shard_map/reduce_scatter | solution.py:60
  163.9 18.3 %copy-start = (bf16[8,128,1024]{2,1,0:T(8,128)(2,1)S(1)}, bf16[8,128,1024]{2,1,0:T(8,128)(2,1)}, u32[]{:S(2)}) copy-start(bf16[8,128,1024]{2,1,0:T(8,128)(2,1)} %copy.8) | copy-start | bytes 6291460
  163.9 108.7 %reduce-scatter.5.cloned.1.call-start = ((), (), s32[]{:S(2)}) async-start(), calls=%async_computation.6 | async-start | bytes 2359296 | tf_op jit(solution)/shard_map/reduce_scatter | solution.py:63
Sparse Core Ops, SparseCore 0:
  23.3 134.6 all-gather.1
  164.0 64.7 reduce-scatter.2
  232.3 40.2 reduce-scatter.4
